TPU v7x, 32 devices: a whole 2x2x4 slice. The times are simulated.
32 devices in a mesh: grp: 2 (over y), skill: 16 (over z, x, core).
Axes of the slice: x: 2, y: 2, z: 4, core: 2. Of those that a mesh axis runs over, the one named last changes fastest.
Arguments:
- value_next: bfloat16 [2048, 4, 2048], P('skill', 'grp'), parts along dimension 1, may hold values from -6 to 6
- income_matrix: float32 [64, 32], P('grp'), parts along dimension 0, may hold values from -1 to 1
- block_weights: bfloat16 [16, 16, 4, 128, 128], P('skill')
- block_offset: int32 [16, 16, 4], P('skill'), may hold values from 0 to 3, as said below
- block_count: int32 [16, 16], P('skill'), may hold values from 1 to 4, as said below
- asset_next: int32 [16, 2, 2048], replicated, may hold values from 0 to 1
- flow: float32 [32, 2, 2048], P('grp'), parts along dimension 0, may hold values from -4 to 15
Outputs:
- value_now: bfloat16 [2048, 4, 2048], P('skill', 'grp'), parts along dimension 1
There are 2 independent parts, one for each index of `grp`. A program takes and returns all parts, laid end to end along the dimension named above; an argument that names none is the same for every part. Nothing has to cross between parts.
Inputs may be any that keep to these rules, and one draw needn't show every extreme that they name: `block_offset`: each row of 4 entries is a permutation of 0 to 3, the same for every level. `block_count`: the same for every level.
All inputs are finite; a program needn't handle non-finite values.
Results may differ from a plain program's by a relative error of at most 0.0031.
Values may be sent and summed in bfloat16 or wider, within the bound.
A program may use at most 128 MiB of HBM per device.

v0:
```python
import jax
import jax.numpy as jnp
from jax import lax
from jax.sharding import PartitionSpec as P


def shifted(block, axis, distance):
    devices = range(lax.axis_size(axis))
    route = [(i - distance, i) for i in devices if i - distance in devices]
    return lax.ppermute(block, axis, route)


def on_device(
    value_next, income_matrix, block_weights, block_offset, block_count, asset_next, flow
):
    tiles = lax.axis_size("skill")
    local_rows, assets, skills = value_next.shape
    tile = skills // tiles
    rows = local_rows * tiles
    shocks = income_matrix.shape[0]
    parents = rows // shocks
    blocks = block_offset.shape[-1]
    levels = block_offset.shape[1]
    arrived = lax.all_to_all(value_next, "skill", split_axis=2, concat_axis=0, tiled=True)
    width = arrived.shape[2]
    grid = arrived.astype(jnp.float32).reshape(parents, shocks, assets * width)
    mixed = jnp.einsum("fe,hex->hfx", income_matrix, grid, precision=lax.Precision.HIGHEST)
    own_tile = mixed.reshape(rows, assets, width).astype(jnp.bfloat16)
    gathered = [own_tile]
    for step in range(1, blocks):
        gathered.append(shifted(own_tile, "skill", -step))
    window = jnp.concatenate(gathered, axis=2)
    matrix = window.reshape(rows * assets, blocks * tile)
    place = jnp.arange(blocks, dtype=jnp.int32)
    offsets = block_offset[0]
    counts = block_count[0]
    select = (
        (offsets[:, :, None] == place[None, None, :])
        & (place[None, :, None] < counts[:, None, None])
    ).astype(jnp.float32)
    transit = jnp.einsum("ikr,ikst->irts", select, block_weights[0].astype(jnp.float32))
    transit = transit.astype(jnp.bfloat16).reshape(levels, blocks * tile, tile)
    flow_rows = jnp.transpose(flow, (0, 2, 1))[..., None]
    choose = jnp.transpose(asset_next, (0, 2, 1))

    def level_step(index, carry):
        running_max, running_total = carry
        cont = jnp.dot(matrix, transit[index], preferred_element_type=jnp.float32).reshape(
            rows, assets, tile
        )
        chosen = choose[index][:, :, None]
        picked = jnp.zeros((rows, assets, tile), jnp.float32)
        for option in range(assets):
            picked = picked + jnp.where(chosen == option, cont[:, option : option + 1, :], 0.0)
        score = (flow_rows[index] + 0.96 * picked) / 0.05
        new_max = jnp.maximum(running_max, score)
        new_total = running_total * jnp.exp(running_max - new_max) + jnp.exp(score - new_max)
        return (new_max, new_total)

    start_max = jnp.full((rows, assets, tile), -jnp.inf, jnp.float32)
    start_total = jnp.zeros((rows, assets, tile), jnp.float32)
    final_max, final_total = lax.fori_loop(0, levels, level_step, (start_max, start_total))
    value_tile = (0.05 * (final_max + jnp.log(final_total))).astype(jnp.bfloat16)
    return lax.all_to_all(value_tile, "skill", split_axis=0, concat_axis=2, tiled=True)


def solution(mesh):
    placed = (
        P("skill", "grp", None),
        P("grp", None),
        P("skill", None, None, None, None),
        P("skill", None, None),
        P("skill", None),
        P(),
        P("grp", None, None),
    )
    return jax.shard_map(
        on_device, mesh=mesh, in_specs=placed, out_specs=P("skill", "grp", None), check_vma=False
    )
```

profile of v0, /device:TPU:16, one launch (start us, length us, event | category | flops | bytes accessed | tf_op | source)
XLA Modules:
  0.0 644.6 jit_solution(14439508790451273633)
XLA Ops:
  0.0 4.9 copy.39
  4.9 31.2 %all_to_all.33 = bf16[128,2,2048]{0,1,2:T(2,128)(2,1)S(1)} all-to-all(bf16[128,2,2048]{0,1,2:T(2,128)(2,1)} %copy.39), channel_id=1, replica_groups=mesh['grp'=2,'skill'=16] {'skill'}, dimensions={2} | all-to-all | bytes 2097152 | tf_op jit(solution)/shard_map/all_to_all | solution.py:24
  36.2 3.8 copy.40
  45.0 2.4 collective-permute-start.2
  47.5 2.9 collective-permute-start.1
  52.8 3.1 convert_bitcast_fusion
  55.9 4.2 copy.44
  60.1 8.6 %copy.36 = s32[16,2,2048]{1,2,0:T(8,128)} copy(s32[16,2,2048]{2,1,0:T(2,128)S(1)} %copy-done.3) | data formatting | bytes 524288 | tf_op args[5]
  68.7 8.6 %copy.35 = f32[16,2,2048]{1,2,0:T(8,128)} copy(f32[16,2,2048]{2,1,0:T(2,128)S(1)} %copy-done.4) | data formatting | bytes 524288 | tf_op args[6]
  77.3 15.9 %collective-permute-done.1 = bf16[2048,2,128]{2,1,0:T(2,128)(2,1)} collective-permute-done((bf16[2048,2,128]{2,1,0:T(2,128)(2,1)S(1)}, bf16[2048,2,128]{2,1,0:T(2,128)(2,1)}, u32[]{:S(2)}, u32[]{:S(2)}) %collective-permute-start.1) | collective-permute-done | bytes 1048608 | tf_op jit(solution)/shard_map/ppermute | solution.py:10
  93.2 11.2 %collective-permute-done = bf16[2048,2,128]{2,1,0:T(2,128)(2,1)} collective-permute-done((bf16[2048,2,128]{2,1,0:T(2,128)(2,1)S(1)}, bf16[2048,2,128]{2,1,0:T(2,128)(2,1)}, u32[]{:S(2)}, u32[]{:S(2)}) %collective-permute-start) | collective-permute-done | bytes 1048608 | tf_op jit(solution)/shard_map/ppermute | solution.py:10
  104.5 8.8 %pad_maximum_fusion = bf16[2048,2,512]{2,1,0:T(2,128)(2,1)} fusion(bf16[2048,2,128]{2,1,0:T(2,128)(2,1)} %collective-permute-done.2, bf16[2048,2,128]{2,1,0:T(2,128)(2,1)} %collective-permute-done.1, bf16[2048,2,128]{2,1,0:T(2,128)(2,1)} %collective-permute-done, bf16[2048,2,128]{2,1,0:T(2,128)(2,1)S(1)} %convert_element_type.25), kind=kLoop, calls=%fused_computation.12 | loop fusion | flops 16777216 | bytes 8388608 | tf_op jit(solution)/shard_map/concatenate | solution.py:32
  113.2 7.2 %reshape.73 = bf16[4096,512]{1,0:T(8,128)(2,1)} reshape(bf16[2048,2,512]{2,1,0:T(2,128)(2,1)} %pad_maximum_fusion) | data formatting | bytes 8388608 | tf_op jit(solution)/shard_map/reshape | solution.py:33
  120.4 487.8 %while.16 = (s32[]{:T(128)}, f32[2048,2,128]{2,1,0:T(2,128)}, f32[2048,2,128]{2,1,0:T(2,128)}, f32[16,2048,2,1]{2,1,3,0:T(8,128)}, s32[16,2048,2]{2,1,0:T(8,128)...) while((s32[]{:T(128)}, f32[2048,2,128]{2,1,0:T(2,128)}, ...), condition=%wide.region_1.2_spmd.clone, body=%wide.region_0.1_spmd.clone.sunk | while | flops 543694848 | bytes 25395352 | solution.py:62
  123.9 3.8 convolution_bitcast_fusion.2
  129.5 3.9 fusion.26
  133.4 16.8 %fusion.27 = (f32[2048,2,128]{2,1,0:T(2,128)}, f32[2048,2,128]{2,1,0:T(2,128)}) fusion(f32[2048,2,128]{2,1,0:T(2,128)} %get-tuple-element.270, pred[]{:T(512)S(6)} %compare.3, f32[2048,2,128]{2,1,0:T(2,128)} %get-tuple-element.269, f32[2048,128]{1,0:T(8,128)S(1)} %bitcast.63, pred[2048,2]{1,0:T(8,128)(4,1)S(1)} %copy-done.2, ...), kind=kLoop, calls=%fused_computation.2.clone.1 | loop fusion | flops 6815744 | bytes 10510337 | tf_op jit(solution)/shard_map/while/body/eval_jaxpr/add | solution.py:57
  153.7 3.8 convolution_bitcast_fusion.2
  159.3 3.9 fusion.26
  163.3 17.5 %fusion.27 = (f32[2048,2,128]{2,1,0:T(2,128)}, f32[2048,2,128]{2,1,0:T(2,128)}) fusion(f32[2048,2,128]{2,1,0:T(2,128)} %get-tuple-element.270, pred[]{:T(512)S(6)} %compare.3, f32[2048,2,128]{2,1,0:T(2,128)} %get-tuple-element.269, f32[2048,128]{1,0:T(8,128)S(1)} %bitcast.63, pred[2048,2]{1,0:T(8,128)(4,1)S(1)} %copy-done.2, ...), kind=kLoop, calls=%fused_computation.2.clone.1 | loop fusion | flops 6815744 | bytes 10510337 | tf_op jit(solution)/shard_map/while/body/eval_jaxpr/add | solution.py:57
  184.3 3.8 convolution_bitcast_fusion.2
  189.9 3.9 fusion.26
  193.8 17.5 %fusion.27 = (f32[2048,2,128]{2,1,0:T(2,128)}, f32[2048,2,128]{2,1,0:T(2,128)}) fusion(f32[2048,2,128]{2,1,0:T(2,128)} %get-tuple-element.270, pred[]{:T(512)S(6)} %compare.3, f32[2048,2,128]{2,1,0:T(2,128)} %get-tuple-element.269, f32[2048,128]{1,0:T(8,128)S(1)} %bitcast.63, pred[2048,2]{1,0:T(8,128)(4,1)S(1)} %copy-done.2, ...), kind=kLoop, calls=%fused_computation.2.clone.1 | loop fusion | flops 6815744 | bytes 10510337 | tf_op jit(solution)/shard_map/while/body/eval_jaxpr/add | solution.py:57
  214.8 3.8 convolution_bitcast_fusion.2
  220.4 3.9 fusion.26
  224.3 17.5 %fusion.27 = (f32[2048,2,128]{2,1,0:T(2,128)}, f32[2048,2,128]{2,1,0:T(2,128)}) fusion(f32[2048,2,128]{2,1,0:T(2,128)} %get-tuple-element.270, pred[]{:T(512)S(6)} %compare.3, f32[2048,2,128]{2,1,0:T(2,128)} %get-tuple-element.269, f32[2048,128]{1,0:T(8,128)S(1)} %bitcast.63, pred[2048,2]{1,0:T(8,128)(4,1)S(1)} %copy-done.2, ...), kind=kLoop, calls=%fused_computation.2.clone.1 | loop fusion | flops 6815744 | bytes 10510337 | tf_op jit(solution)/shard_map/while/body/eval_jaxpr/add | solution.py:57
  245.4 3.8 convolution_bitcast_fusion.2
  250.9 3.9 fusion.26
  254.9 17.5 %fusion.27 = (f32[2048,2,128]{2,1,0:T(2,128)}, f32[2048,2,128]{2,1,0:T(2,128)}) fusion(f32[2048,2,128]{2,1,0:T(2,128)} %get-tuple-element.270, pred[]{:T(512)S(6)} %compare.3, f32[2048,2,128]{2,1,0:T(2,128)} %get-tuple-element.269, f32[2048,128]{1,0:T(8,128)S(1)} %bitcast.63, pred[2048,2]{1,0:T(8,128)(4,1)S(1)} %copy-done.2, ...), kind=kLoop, calls=%fused_computation.2.clone.1 | loop fusion | flops 6815744 | bytes 10510337 | tf_op jit(solution)/shard_map/while/body/eval_jaxpr/add | solution.py:57
  275.9 3.8 convolution_bitcast_fusion.2
  281.5 3.9 fusion.26
  285.4 17.5 %fusion.27 = (f32[2048,2,128]{2,1,0:T(2,128)}, f32[2048,2,128]{2,1,0:T(2,128)}) fusion(f32[2048,2,128]{2,1,0:T(2,128)} %get-tuple-element.270, pred[]{:T(512)S(6)} %compare.3, f32[2048,2,128]{2,1,0:T(2,128)} %get-tuple-element.269, f32[2048,128]{1,0:T(8,128)S(1)} %bitcast.63, pred[2048,2]{1,0:T(8,128)(4,1)S(1)} %copy-done.2, ...), kind=kLoop, calls=%fused_computation.2.clone.1 | loop fusion | flops 6815744 | bytes 10510337 | tf_op jit(solution)/shard_map/while/body/eval_jaxpr/add | solution.py:57
  306.4 3.8 convolution_bitcast_fusion.2
  312.0 3.9 fusion.26
  316.0 17.5 %fusion.27 = (f32[2048,2,128]{2,1,0:T(2,128)}, f32[2048,2,128]{2,1,0:T(2,128)}) fusion(f32[2048,2,128]{2,1,0:T(2,128)} %get-tuple-element.270, pred[]{:T(512)S(6)} %compare.3, f32[2048,2,128]{2,1,0:T(2,128)} %get-tuple-element.269, f32[2048,128]{1,0:T(8,128)S(1)} %bitcast.63, pred[2048,2]{1,0:T(8,128)(4,1)S(1)} %copy-done.2, ...), kind=kLoop, calls=%fused_computation.2.clone.1 | loop fusion | flops 6815744 | bytes 10510337 | tf_op jit(solution)/shard_map/while/body/eval_jaxpr/add | solution.py:57
  337.0 3.8 convolution_bitcast_fusion.2
  342.5 3.9 fusion.26
  346.5 17.5 %fusion.27 = (f32[2048,2,128]{2,1,0:T(2,128)}, f32[2048,2,128]{2,1,0:T(2,128)}) fusion(f32[2048,2,128]{2,1,0:T(2,128)} %get-tuple-element.270, pred[]{:T(512)S(6)} %compare.3, f32[2048,2,128]{2,1,0:T(2,128)} %get-tuple-element.269, f32[2048,128]{1,0:T(8,128)S(1)} %bitcast.63, pred[2048,2]{1,0:T(8,128)(4,1)S(1)} %copy-done.2, ...), kind=kLoop, calls=%fused_computation.2.clone.1 | loop fusion | flops 6815744 | bytes 10510337 | tf_op jit(solution)/shard_map/while/body/eval_jaxpr/add | solution.py:57
  367.5 3.8 convolution_bitcast_fusion.2
  373.1 3.9 fusion.26
  377.0 17.5 %fusion.27 = (f32[2048,2,128]{2,1,0:T(2,128)}, f32[2048,2,128]{2,1,0:T(2,128)}) fusion(f32[2048,2,128]{2,1,0:T(2,128)} %get-tuple-element.270, pred[]{:T(512)S(6)} %compare.3, f32[2048,2,128]{2,1,0:T(2,128)} %get-tuple-element.269, f32[2048,128]{1,0:T(8,128)S(1)} %bitcast.63, pred[2048,2]{1,0:T(8,128)(4,1)S(1)} %copy-done.2, ...), kind=kLoop, calls=%fused_computation.2.clone.1 | loop fusion | flops 6815744 | bytes 10510337 | tf_op jit(solution)/shard_map/while/body/eval_jaxpr/add | solution.py:57
  398.0 3.8 convolution_bitcast_fusion.2
  403.6 3.9 fusion.26
  407.6 17.5 %fusion.27 = (f32[2048,2,128]{2,1,0:T(2,128)}, f32[2048,2,128]{2,1,0:T(2,128)}) fusion(f32[2048,2,128]{2,1,0:T(2,128)} %get-tuple-element.270, pred[]{:T(512)S(6)} %compare.3, f32[2048,2,128]{2,1,0:T(2,128)} %get-tuple-element.269, f32[2048,128]{1,0:T(8,128)S(1)} %bitcast.63, pred[2048,2]{1,0:T(8,128)(4,1)S(1)} %copy-done.2, ...), kind=kLoop, calls=%fused_computation.2.clone.1 | loop fusion | flops 6815744 | bytes 10510337 | tf_op jit(solution)/shard_map/while/body/eval_jaxpr/add | solution.py:57
  428.6 3.8 convolution_bitcast_fusion.2
  434.1 3.9 fusion.26
  438.1 17.5 %fusion.27 = (f32[2048,2,128]{2,1,0:T(2,128)}, f32[2048,2,128]{2,1,0:T(2,128)}) fusion(f32[2048,2,128]{2,1,0:T(2,128)} %get-tuple-element.270, pred[]{:T(512)S(6)} %compare.3, f32[2048,2,128]{2,1,0:T(2,128)} %get-tuple-element.269, f32[2048,128]{1,0:T(8,128)S(1)} %bitcast.63, pred[2048,2]{1,0:T(8,128)(4,1)S(1)} %copy-done.2, ...), kind=kLoop, calls=%fused_computation.2.clone.1 | loop fusion | flops 6815744 | bytes 10510337 | tf_op jit(solution)/shard_map/while/body/eval_jaxpr/add | solution.py:57
  459.1 3.8 convolution_bitcast_fusion.2
  464.7 3.9 fusion.26
  468.6 17.5 %fusion.27 = (f32[2048,2,128]{2,1,0:T(2,128)}, f32[2048,2,128]{2,1,0:T(2,128)}) fusion(f32[2048,2,128]{2,1,0:T(2,128)} %get-tuple-element.270, pred[]{:T(512)S(6)} %compare.3, f32[2048,2,128]{2,1,0:T(2,128)} %get-tuple-element.269, f32[2048,128]{1,0:T(8,128)S(1)} %bitcast.63, pred[2048,2]{1,0:T(8,128)(4,1)S(1)} %copy-done.2, ...), kind=kLoop, calls=%fused_computation.2.clone.1 | loop fusion | flops 6815744 | bytes 10510337 | tf_op jit(solution)/shard_map/while/body/eval_jaxpr/add | solution.py:57
  489.6 3.8 convolution_bitcast_fusion.2
  495.2 3.9 fusion.26
  499.2 17.5 %fusion.27 = (f32[2048,2,128]{2,1,0:T(2,128)}, f32[2048,2,128]{2,1,0:T(2,128)}) fusion(f32[2048,2,128]{2,1,0:T(2,128)} %get-tuple-element.270, pred[]{:T(512)S(6)} %compare.3, f32[2048,2,128]{2,1,0:T(2,128)} %get-tuple-element.269, f32[2048,128]{1,0:T(8,128)S(1)} %bitcast.63, pred[2048,2]{1,0:T(8,128)(4,1)S(1)} %copy-done.2, ...), kind=kLoop, calls=%fused_computation.2.clone.1 | loop fusion | flops 6815744 | bytes 10510337 | tf_op jit(solution)/shard_map/while/body/eval_jaxpr/add | solution.py:57
  520.2 3.8 convolution_bitcast_fusion.2
  525.7 3.9 fusion.26
  529.7 17.5 %fusion.27 = (f32[2048,2,128]{2,1,0:T(2,128)}, f32[2048,2,128]{2,1,0:T(2,128)}) fusion(f32[2048,2,128]{2,1,0:T(2,128)} %get-tuple-element.270, pred[]{:T(512)S(6)} %compare.3, f32[2048,2,128]{2,1,0:T(2,128)} %get-tuple-element.269, f32[2048,128]{1,0:T(8,128)S(1)} %bitcast.63, pred[2048,2]{1,0:T(8,128)(4,1)S(1)} %copy-done.2, ...), kind=kLoop, calls=%fused_computation.2.clone.1 | loop fusion | flops 6815744 | bytes 10510337 | tf_op jit(solution)/shard_map/while/body/eval_jaxpr/add | solution.py:57
  550.7 3.8 convolution_bitcast_fusion.2
  556.3 3.9 fusion.26
  560.2 17.5 %fusion.27 = (f32[2048,2,128]{2,1,0:T(2,128)}, f32[2048,2,128]{2,1,0:T(2,128)}) fusion(f32[2048,2,128]{2,1,0:T(2,128)} %get-tuple-element.270, pred[]{:T(512)S(6)} %compare.3, f32[2048,2,128]{2,1,0:T(2,128)} %get-tuple-element.269, f32[2048,128]{1,0:T(8,128)S(1)} %bitcast.63, pred[2048,2]{1,0:T(8,128)(4,1)S(1)} %copy-done.2, ...), kind=kLoop, calls=%fused_computation.2.clone.1 | loop fusion | flops 6815744 | bytes 10510337 | tf_op jit(solution)/shard_map/while/body/eval_jaxpr/add | solution.py:57
  581.2 3.8 convolution_bitcast_fusion.2
  586.8 3.9 fusion.26
  590.8 17.5 %fusion.27 = (f32[2048,2,128]{2,1,0:T(2,128)}, f32[2048,2,128]{2,1,0:T(2,128)}) fusion(f32[2048,2,128]{2,1,0:T(2,128)} %get-tuple-element.270, pred[]{:T(512)S(6)} %compare.3, f32[2048,2,128]{2,1,0:T(2,128)} %get-tuple-element.269, f32[2048,128]{1,0:T(8,128)S(1)} %bitcast.63, pred[2048,2]{1,0:T(8,128)(4,1)S(1)} %copy-done.2, ...), kind=kLoop, calls=%fused_computation.2.clone.1 | loop fusion | flops 6815744 | bytes 10510337 | tf_op jit(solution)/shard_map/while/body/eval_jaxpr/add | solution.py:57
  608.3 3.4 multiply_convert_fusion
  611.7 30.6 %all_to_all.34 = bf16[2048,2,128]{2,1,0:T(2,128)(2,1)S(1)} all-to-all(bf16[2048,2,128]{2,1,0:T(2,128)(2,1)S(1)} %multiply_convert_fusion), channel_id=1, replica_groups=mesh['grp'=2,'skill'=16] {'skill'}, dimensions={0} | all-to-all | bytes 2097152 | tf_op jit(solution)/shard_map/all_to_all | solution.py:64
  (105 shorter events, 94.7 us)
Async XLA Ops:
  0.0 52.8 %copy-start = (bf16[1,16,4,128,128]{4,3,2,1,0:T(8,128)(2,1)S(1)}, bf16[1,16,4,128,128]{4,3,2,1,0:T(8,128)(2,1)}, u32[]{:S(2)}) copy-start(bf16[1,16,4,128,128]{4,3,2,1,0:T(8,128)(2,1)} %param.11) | copy-start | bytes 6291460
  36.2 5.5 copy-start.5
  41.7 10.9 %copy-start.6 = (s32[1,16,4]{1,2,0:T(4,128)S(1)}, s32[1,16,4]{1,2,0:T(4,128)}, u32[]{:S(2)}) copy-start(s32[1,16,4]{1,2,0:T(4,128)} %param.12) | copy-start | bytes 772
  41.7 11.0 %copy-start.7 = (s32[1,16]{1,0:T(1,128)S(1)}, s32[1,16]{1,0:T(1,128)}, u32[]{:S(2)}) copy-start(s32[1,16]{1,0:T(1,128)} %param.13) | copy-start | bytes 196
  45.0 32.3 %collective-permute-start.2 = (bf16[2048,2,128]{2,1,0:T(2,128)(2,1)S(1)}, bf16[2048,2,128]{2,1,0:T(2,128)(2,1)}, u32[]{:S(2)}, u32[]{:S(2)}) collective-permute-start(bf16[2048,2,128]{2,1,0:T(2,128)(2,1)S(1)} %convert_element_type.25), channel_id=1, source_target_pairs={{3,0},{4,1},{5,2},{6,3},{7,4},{8,5},{9,6},{10,7},{11,8},{12,9},{13... | collective-permute-start | bytes 3145736 | tf_op jit(solution)/shard_map/ppermute | solution.py:10
  47.5 45.8 %collective-permute-start.1 = (bf16[2048,2,128]{2,1,0:T(2,128)(2,1)S(1)}, bf16[2048,2,128]{2,1,0:T(2,128)(2,1)}, u32[]{:S(2)}, u32[]{:S(2)}) collective-permute-start(bf16[2048,2,128]{2,1,0:T(2,128)(2,1)S(1)} %convert_element_type.25), channel_id=1, source_target_pairs={{2,0},{3,1},{4,2},{5,3},{6,4},{7,5},{8,6},{9,7},{10,8},{11,9},{12,... | collective-permute-start | bytes 3145736 | tf_op jit(solution)/shard_map/ppermute | solution.py:10
  50.3 54.1 %collective-permute-start = (bf16[2048,2,128]{2,1,0:T(2,128)(2,1)S(1)}, bf16[2048,2,128]{2,1,0:T(2,128)(2,1)}, u32[]{:S(2)}, u32[]{:S(2)}) collective-permute-start(bf16[2048,2,128]{2,1,0:T(2,128)(2,1)S(1)} %convert_element_type.25), channel_id=1, source_target_pairs={{1,0},{2,1},{3,2},{4,3},{5,4},{6,5},{7,6},{8,7},{9,8},{10,9},{11,1... | collective-permute-start | bytes 3145736 | tf_op jit(solution)/shard_map/ppermute | solution.py:10
  55.9 4.2 copy-start.3
  60.1 8.6 %copy-start.4 = (f32[16,2,2048]{2,1,0:T(2,128)S(1)}, f32[16,2,2048]{2,1,0:T(2,128)}, u32[]{:S(2)}) copy-start(f32[16,2,2048]{2,1,0:T(2,128)} %param.15) | copy-start | bytes 786436
  129.5 3.9 copy-start.2
  159.3 3.9 copy-start.2
  189.9 3.9 copy-start.2
  220.4 3.9 copy-start.2
  250.9 3.9 copy-start.2
  281.5 3.9 copy-start.2
  312.0 3.9 copy-start.2
  342.5 3.9 copy-start.2
  373.1 3.9 copy-start.2
  403.6 3.9 copy-start.2
  434.1 3.9 copy-start.2
  464.7 3.9 copy-start.2
  495.2 3.9 copy-start.2
  525.7 3.9 copy-start.2
  556.3 3.9 copy-start.2
  586.8 3.9 copy-start.2
  642.2 2.3 copy-start.1
where the time goes:
time: 649 us; the launch traced here: 645 us
  other arithmetic  327 us (50%)
  local copies, waits for them, and re-layouts  155 us (24%)
  matrix products  65.2 us (10%)
  blocking collectives  61.8 us (10%)
  waiting for transfers between devices  27.2 us (4%)
  starting transfers between devices  7.57 us (1%)
    add x16, other arithmetic, level_step(): running_total * jnp.exp(running_max - new_max) + jnp.exp(score - new_max)  279 us
    slice x16, local copies, waits for them, and re-layouts, level_step(): cont[:, option:option + 1, :]  62.9 us
    dot_general x16, matrix products, level_step(): jnp.dot(matrix, transit[index], preferred_element_type=jnp.float32)  60.2 us
    eq x16, other arithmetic, level_step(): chosen == option  35.3 us
    all_to_all x1, blocking collectives, on_device(): lax.all_to_all(value_next, 'skill', split_axis=2, concat_axis=0, tiled=True)  31.2 us
    all_to_all x1, blocking collectives, on_device(): lax.all_to_all(value_tile, 'skill', split_axis=0, concat_axis=2, tiled=True)  30.6 us
    dot_general x16, local copies, waits for them, and re-layouts, level_step(): jnp.dot(matrix, transit[index], preferred_element_type=jnp.float32)  28.9 us
    ppermute x3, waiting for transfers between devices, shifted(): return lax.ppermute(block, axis, route)  27.2 us
  transfers between devices with their start and end apart: 3, of which 2 were waited for; matrix products, arithmetic and copies ran while one was open for 4% of the time, Pallas kernels for 0%

commit v1 on v0

--- a/solution.py
+++ b/solution.py
@@ -1,8 +1,12 @@
+import functools
+import math
+
 import jax
 import jax.numpy as jnp
 from jax import lax
+from jax.experimental import pallas as pl
+from jax.experimental.pallas import tpu as pltpu
 from jax.sharding import PartitionSpec as P
-
 
 def shifted(block, axis, distance):
     devices = range(lax.axis_size(axis))
@@ -10,7 +14,7 @@
     return lax.ppermute(block, axis, route)
 
 
-def on_device(
+def on_device_split(
     value_next, income_matrix, block_weights, block_offset, block_count, asset_next, flow
 ):
     tiles = lax.axis_size("skill")
@@ -64,6 +68,154 @@
     return lax.all_to_all(value_tile, "skill", split_axis=0, concat_axis=2, tiled=True)
 
 
+SUB = 16
+STEP = 32
+SCALE = math.log2(math.e) / 0.05
+
+
+def split_three(mix):
+    high = mix.astype(jnp.bfloat16)
+    rest = mix - high.astype(jnp.float32)
+    middle = rest.astype(jnp.bfloat16)
+    low = (rest - middle.astype(jnp.float32)).astype(jnp.bfloat16)
+    return high, middle, low
+
+
+def arrange_weights(t, tiles, weights, offsets, counts, sorted_weights):
+    levels, blocks, tile, _ = weights.shape
+
+    def one_level(i, carry):
+        for r in range(blocks):
+            total = jnp.zeros((tile, tile), jnp.float32)
+            for k in range(blocks):
+                live = (offsets[k] == r) & (counts > k) & (t + r < tiles)
+                total = total + jnp.where(live, weights[i, k].astype(jnp.float32), 0.0)
+            total = total.astype(jnp.bfloat16)
+            for q in range(tile // STEP):
+                sorted_weights[q, pl.ds(pl.multiple_of(i * STEP, STEP), STEP), r * tile : (r + 1) * tile] = total[
+                    q * STEP : (q + 1) * STEP
+                ]
+        return carry
+
+    lax.fori_loop(0, levels, one_level, 0)
+
+
+def one_chunk(window, flow, choose, sorted_weights, scaled, chosen, cont, value, levels, rows):
+    for a in range(2):
+        scaled[a] = flow[:, a, :] * SCALE
+        chosen[a] = choose[:, a, :]
+    steps = sorted_weights.shape[0]
+
+    def multiply(q):
+        cont[q % 2] = lax.dot_general(
+            sorted_weights[q], window, (((1,), (1,)), ((), ())), preferred_element_type=jnp.float32
+        )
+
+    def reduce(q):
+        for part in range(STEP // SUB):
+            for a in range(2):
+                scores = []
+                for i in range(levels):
+                    at = i * STEP + part * SUB
+                    first = cont[q % 2, at : at + SUB, :rows]
+                    second = cont[q % 2, at : at + SUB, rows:]
+                    picked = jnp.where(chosen[a, i : i + 1, :] == 1, second, first)
+                    scores.append(scaled[a, i : i + 1, :] + (0.96 * SCALE) * picked)
+                top = scores
+                while len(top) > 1:
+                    top = [jnp.maximum(x, y) for x, y in zip(top[::2], top[1::2])]
+                terms = [jnp.exp2(x - top[0]) for x in scores]
+                while len(terms) > 1:
+                    terms = [x + y for x, y in zip(terms[::2], terms[1::2])]
+                start = q * STEP + part * SUB
+                value[a, start : start + SUB, :] = (1.0 / SCALE) * (top[0] + jnp.log2(terms[0]))
+
+    multiply(0)
+    for q in range(steps):
+        if q + 1 < steps:
+            multiply(q + 1)
+        reduce(q)
+
+def mix_kernel(mix, values, out):
+    tile = out.shape[-1]
+    parts = split_three(mix[...])
+    for t in range(out.shape[0]):
+        block = values[:, t * tile : (t + 1) * tile]
+        total = jnp.dot(parts[2], block, preferred_element_type=jnp.float32)
+        total = total + jnp.dot(parts[1], block, preferred_element_type=jnp.float32)
+        total = total + jnp.dot(parts[0], block, preferred_element_type=jnp.float32)
+        out[t, 0] = total.astype(jnp.bfloat16)
+
+
+def level_kernel(
+    tiles, offsets, counts, weights, flow, choose, w0, w1, w2, w3, out, sorted_weights, scaled, chosen, cont, value
+):
+    levels = weights.shape[0]
+    rows = w0.shape[2]
+    tile = w0.shape[3]
+
+    @pl.when(pl.program_id(0) == 0)
+    def _():
+        t = lax.axis_index("skill")
+        arrange_weights(t, tiles, weights, [offsets[0, k] for k in range(4)], counts[0, 0], sorted_weights)
+
+    window = jnp.concatenate([w[0].reshape(2 * rows, tile) for w in (w0, w1, w2, w3)], axis=1)
+    one_chunk(window, flow[...], choose[...], sorted_weights, scaled, chosen, cont, value, levels, rows)
+    for a in range(2):
+        out[0, a] = value[a].T.astype(jnp.bfloat16)
+
+
+def on_device(value_next, income_matrix, block_weights, block_offset, block_count, asset_next, flow):
+    tiles = lax.axis_size("skill")
+    rows, assets, skills = value_next.shape
+    tile = skills // tiles
+    shocks = income_matrix.shape[0]
+    levels, blocks = block_weights.shape[1:3]
+    mix = jnp.kron(jnp.eye(rows // shocks, dtype=jnp.float32), income_matrix)
+    turned = jnp.transpose(value_next, (1, 0, 2))
+    expected = pl.pallas_call(
+        mix_kernel,
+        out_shape=jax.ShapeDtypeStruct((tiles, assets, rows, tile), jnp.bfloat16),
+        grid=(assets,),
+        in_specs=[
+            pl.BlockSpec((rows, rows), lambda a: (0, 0)),
+            pl.BlockSpec((None, rows, skills), lambda a: (a, 0, 0)),
+        ],
+        out_specs=pl.BlockSpec((tiles, 1, rows, tile), lambda a: (0, a, 0, 0)),
+    )(mix, turned)
+    own = lax.all_to_all(expected, "skill", split_axis=0, concat_axis=0, tiled=True)
+    window = [own] + [shifted(own, "skill", -step) for step in range(1, blocks)]
+    chunk = pl.BlockSpec((1, assets, rows, tile), lambda n: (n, 0, 0, 0))
+    per_row = pl.BlockSpec((levels, assets, rows), lambda n: (0, 0, n))
+    value = pl.pallas_call(
+        functools.partial(level_kernel, tiles),
+        out_shape=jax.ShapeDtypeStruct((tiles, assets, rows, tile), jnp.bfloat16),
+        grid=(tiles,),
+        in_specs=[
+            pl.BlockSpec(memory_space=pltpu.SMEM),
+            pl.BlockSpec(memory_space=pltpu.SMEM),
+            pl.BlockSpec((levels, blocks, tile, tile), lambda n: (0, 0, 0, 0)),
+            per_row,
+            per_row,
+            chunk,
+            chunk,
+            chunk,
+            chunk,
+        ],
+        out_specs=chunk,
+        scratch_shapes=[
+            pltpu.VMEM((tile // STEP, levels * STEP, blocks * tile), jnp.bfloat16),
+            pltpu.VMEM((assets, levels, rows), jnp.float32),
+            pltpu.VMEM((assets, levels, rows), jnp.int32),
+            pltpu.VMEM((2, levels * STEP, assets * rows), jnp.float32),
+            pltpu.VMEM((assets, tile, rows), jnp.float32),
+        ],
+        compiler_params=pltpu.CompilerParams(vmem_limit_bytes=48 * 1024 * 1024),
+    )(block_offset[0], block_count, block_weights[0], flow, asset_next, *window)
+    back = lax.all_to_all(value, "skill", split_axis=0, concat_axis=0, tiled=True)
+    return jnp.transpose(back, (2, 1, 0, 3)).reshape(rows, assets, skills)
+
+
 def solution(mesh):
     placed = (
         P("skill", "grp", None),
@@ -74,6 +226,11 @@
         P(),
         P("grp", None, None),
     )
+
+    def body(value_next, income_matrix, *rest):
+        whole = value_next.shape[0] % income_matrix.shape[0] == 0
+        return (on_device if whole else on_device_split)(value_next, income_matrix, *rest)
+
     return jax.shard_map(
-        on_device, mesh=mesh, in_specs=placed, out_specs=P("skill", "grp", None), check_vma=False
+        body, mesh=mesh, in_specs=placed, out_specs=P("skill", "grp", None), check_vma=False
     )

time: 649 us -> 156 us (0.24)
  other arithmetic: 327 us -> 0.82 us
  local copies, waits for them, and re-layouts: 155 us -> 7.04 us
  matrix products: 65.2 us -> 0 us
  Pallas kernels: 0 us -> 25.4 us
  waiting for transfers between devices: 27.2 us -> 51.8 us
    add x16 -> x0, other arithmetic: 279 us -> none  [level_step(): running_total * jnp.exp(running_max - new_max) + jnp.exp(score - new_max)]
    dot_general x18 -> x0, matrix products: 65.2 us -> none  [the longest x16 60.2 us: level_step(): jnp.dot(matrix, transit[index], preferred_element_type=jnp.float32)]
    slice x16 -> x0, local copies, waits for them, and re-layouts: 62.9 us -> none  [level_step(): cont[:, option:option + 1, :]]
    eq x16 -> x0, other arithmetic: 35.3 us -> none  [level_step(): chosen == option]
    dot_general x16 -> x0, local copies, waits for them, and re-layouts: 28.9 us -> none  [level_step(): jnp.dot(matrix, transit[index], preferred_element_type=jnp.float32)]
    pallas_call x0 -> x2, Pallas kernels: none -> 25.4 us  [the longest x1 22.3 us: on_device(): pl.pallas_call(functools.partial(level_kernel, tiles), out_shape=jax.Shap...]
    ppermute x3, waiting for transfers between devices: 27.2 us -> 51.8 us  [shifted(): return lax.ppermute(block, axis, route)]
    unnamed x18 -> x9, local copies, waits for them, and re-layouts: 26.4 us -> 3.51 us
  transfers between devices with their start and end apart: 3 -> 3, of which waited for: 2 -> 3; matrix products, arithmetic and copies ran while one was open for 4% -> 0% of each run, Pallas kernels for 0% -> 0%
where the time goes in v1:
time: 156 us; the launch traced here: 154 us
  blocking collectives  61.8 us (40%)
  waiting for transfers between devices  51.8 us (33%)
  Pallas kernels  25.4 us (16%)
  starting transfers between devices  7.56 us (5%)
  local copies, waits for them, and re-layouts  7.04 us (5%)
    ppermute x3, waiting for transfers between devices, shifted(): return lax.ppermute(block, axis, route)  51.8 us
    all_to_all x1, blocking collectives, on_device(): lax.all_to_all(expected, 'skill', split_axis=0, concat_axis=0, tiled=True)  31.3 us
    all_to_all x1, blocking collectives, on_device(): lax.all_to_all(value, 'skill', split_axis=0, concat_axis=0, tiled=True)  30.6 us
    pallas_call x1, Pallas kernels, on_device(): pl.pallas_call(functools.partial(level_kernel, tiles), out_shape=jax.Shap...  22.3 us
    ppermute x3, starting transfers between devices, shifted(): return lax.ppermute(block, axis, route)  7.56 us
    unnamed x9, local copies, waits for them, and re-layouts  3.51 us
  transfers between devices with their start and end apart: 3, of which 3 were waited for; matrix products, arithmetic and copies ran while one was open for 0% of the time, Pallas kernels for 0%

profile of v1, /device:TPU:16, one launch (start us, length us, event | category | flops | bytes accessed | tf_op | source)
XLA Modules:
  0.0 154.5 jit_solution(4535063443941669055)
XLA Ops:
  0.0 0.8 broadcast_multiply_fusion
  0.8 0.8 mul.27.mix
  1.6 2.5 %copy.15 = bf16[128,2,2048]{2,0,1:T(8,128)(2,1)} copy(bf16[128,2,2048]{2,1,0:T(2,128)(2,1)} %param.7) | data formatting | bytes 2097152 | tf_op args[0]
  4.2 0.0 copy-start.3
  4.2 0.0 copy-start
  4.2 0.0 copy-start.2
  4.2 3.1 %shard_map.73 = bf16[16,2,128,128]{3,2,1,0:T(8,128)(2,1)} custom-call(f32[128,128]{1,0:T(8,128)} %mul.27.mix, bf16[2,128,2048]{2,1,0:T(8,128)(2,1)} %bitcast.7), custom_call_target="tpu_custom_call" | custom-call | tf_op jit(solution)/shard_map/pallas_call | solution.py:176
  7.2 31.3 %all_to_all.10.w0 = bf16[16,2,128,128]{3,2,1,0:T(8,128)(2,1)S(1)} all-to-all(bf16[16,2,128,128]{3,2,1,0:T(8,128)(2,1)} %shard_map.73), channel_id=1, replica_groups=mesh['grp'=2,'skill'=16] {'skill'}, dimensions={0} | all-to-all | bytes 2097152 | tf_op jit(solution)/shard_map/all_to_all | solution.py:186
  38.5 2.4 %collective-permute-start.2 = (bf16[16,2,128,128]{3,2,1,0:T(8,128)(2,1)S(1)}, bf16[16,2,128,128]{3,2,1,0:T(8,128)(2,1)S(1)}, u32[]{:S(2)}, u32[]{:S(2)}) collective-permute-start(bf16[16,2,128,128]{3,2,1,0:T(8,128)(2,1)S(1)} %all_to_all.10.w0), channel_id=1, source_target_pairs={{3,0},{4,1},{5,2},{6,3},{7,4},{8,5},{9,6},{10,7},{11,8},{12,9},{13... | collective-permute-start | bytes 3145736 | tf_op jit(solution)/shard_map/ppermute | solution.py:14
  40.9 2.9 %collective-permute-start.1 = (bf16[16,2,128,128]{3,2,1,0:T(8,128)(2,1)S(1)}, bf16[16,2,128,128]{3,2,1,0:T(8,128)(2,1)S(1)}, u32[]{:S(2)}, u32[]{:S(2)}) collective-permute-start(bf16[16,2,128,128]{3,2,1,0:T(8,128)(2,1)S(1)} %all_to_all.10.w0), channel_id=1, source_target_pairs={{2,0},{3,1},{4,2},{5,3},{6,4},{7,5},{8,6},{9,7},{10,8},{11,9},{12,... | collective-permute-start | bytes 3145736 | tf_op jit(solution)/shard_map/ppermute | solution.py:14
  43.8 2.2 %collective-permute-start = (bf16[16,2,128,128]{3,2,1,0:T(8,128)(2,1)S(1)}, bf16[16,2,128,128]{3,2,1,0:T(8,128)(2,1)}, u32[]{:S(2)}, u32[]{:S(2)}) collective-permute-start(bf16[16,2,128,128]{3,2,1,0:T(8,128)(2,1)S(1)} %all_to_all.10.w0), channel_id=1, source_target_pairs={{1,0},{2,1},{3,2},{4,3},{5,4},{6,5},{7,6},{8,7},{9,8},{10,9},{11,1... | collective-permute-start | bytes 3145736 | tf_op jit(solution)/shard_map/ppermute | solution.py:14
  46.1 0.0 copy-done.3
  46.1 0.1 copy.11.offsets
  46.2 18.3 %collective-permute-done.2.w3 = bf16[16,2,128,128]{3,2,1,0:T(8,128)(2,1)S(1)} collective-permute-done((bf16[16,2,128,128]{3,2,1,0:T(8,128)(2,1)S(1)}, bf16[16,2,128,128]{3,2,1,0:T(8,128)(2,1)S(1)}, u32[]{:S(2)}, u32[]{:S(2)}) %collective-permute-start.2) | collective-permute-done | bytes 1048608 | tf_op jit(solution)/shard_map/ppermute | solution.py:14
  64.5 22.3 %collective-permute-done.1.w2 = bf16[16,2,128,128]{3,2,1,0:T(8,128)(2,1)S(1)} collective-permute-done((bf16[16,2,128,128]{3,2,1,0:T(8,128)(2,1)S(1)}, bf16[16,2,128,128]{3,2,1,0:T(8,128)(2,1)S(1)}, u32[]{:S(2)}, u32[]{:S(2)}) %collective-permute-start.1) | collective-permute-done | bytes 1048608 | tf_op jit(solution)/shard_map/ppermute | solution.py:14
  86.7 11.2 %collective-permute-done.w1 = bf16[16,2,128,128]{3,2,1,0:T(8,128)(2,1)} collective-permute-done((bf16[16,2,128,128]{3,2,1,0:T(8,128)(2,1)S(1)}, bf16[16,2,128,128]{3,2,1,0:T(8,128)(2,1)}, u32[]{:S(2)}, u32[]{:S(2)}) %collective-permute-start) | collective-permute-done | bytes 1048608 | tf_op jit(solution)/shard_map/ppermute | solution.py:14
  97.9 0.0 copy-done
  98.0 0.0 copy-done.2
  98.0 0.0 copy-start.1
  98.0 0.9 copy-done.1
  98.9 22.3 %shard_map.74 = bf16[16,2,128,128]{3,2,1,0:T(8,128)(2,1)S(1)} custom-call(s32[16,4]{1,0:T(8,128)S(1)} %copy.11.offsets, s32[1,16]{1,0:T(1,128)S(1)} %copy-done.2, bf16[16,4,128,128]{3,2,1,0:T(8,128)(2,1)} %bitcast.10, f32[16,2,2048]{2,1,0:T(2,128)S(1)} %copy-done, s32[16,2,2048]{2,1,0:T(2,128)S(1)} %copy-done.1, ...), custom_call_target="tpu_custom_call" | custom-call | tf_op jit(solution)/shard_map/pallas_call | solution.py:190
  121.2 30.6 %all_to_all.11 = bf16[16,2,128,128]{3,2,1,0:T(8,128)(2,1)S(1)} all-to-all(bf16[16,2,128,128]{3,2,1,0:T(8,128)(2,1)S(1)} %shard_map.74), channel_id=1, replica_groups=mesh['grp'=2,'skill'=16] {'skill'}, dimensions={0} | all-to-all | bytes 2097152 | tf_op jit(solution)/shard_map/all_to_all | solution.py:215
  151.8 0.7 copy.12
  152.4 2.0 %copy.13 = bf16[128,2,2048]{2,1,0:T(2,128)(2,1)} copy(bf16[128,2,2048]{0,2,1:T(8,128)(2,1)S(1)} %bitcast.9) | data formatting | bytes 2097152 | tf_op jit(solution)/shard_map/reshape | solution.py:216
  (1 shorter events, 0.0 us)
Async XLA Ops:
  4.2 41.9 %copy-start.3 = (s32[1,16,4]{1,2,0:T(4,128)S(1)}, s32[1,16,4]{1,2,0:T(4,128)}, u32[]{:S(2)}) copy-start(s32[1,16,4]{1,2,0:T(4,128)} %param.10) | copy-start | bytes 772
  4.2 93.8 %copy-start = (f32[16,2,2048]{2,1,0:T(2,128)S(1)}, f32[16,2,2048]{2,1,0:T(2,128)}, u32[]{:S(2)}) copy-start(f32[16,2,2048]{2,1,0:T(2,128)} %flow.1) | copy-start | bytes 786436
  4.2 93.8 %copy-start.2 = (s32[1,16]{1,0:T(1,128)S(1)}, s32[1,16]{1,0:T(1,128)}, u32[]{:S(2)}) copy-start(s32[1,16]{1,0:T(1,128)} %counts.1) | copy-start | bytes 196
  38.5 26.0 %collective-permute-start.2 = (bf16[16,2,128,128]{3,2,1,0:T(8,128)(2,1)S(1)}, bf16[16,2,128,128]{3,2,1,0:T(8,128)(2,1)S(1)}, u32[]{:S(2)}, u32[]{:S(2)}) collective-permute-start(bf16[16,2,128,128]{3,2,1,0:T(8,128)(2,1)S(1)} %all_to_all.10.w0), channel_id=1, source_target_pairs={{3,0},{4,1},{5,2},{6,3},{7,4},{8,5},{9,6},{10,7},{11,8},{12,9},{13... | collective-permute-start | bytes 3145736 | tf_op jit(solution)/shard_map/ppermute | solution.py:14
  40.9 45.8 %collective-permute-start.1 = (bf16[16,2,128,128]{3,2,1,0:T(8,128)(2,1)S(1)}, bf16[16,2,128,128]{3,2,1,0:T(8,128)(2,1)S(1)}, u32[]{:S(2)}, u32[]{:S(2)}) collective-permute-start(bf16[16,2,128,128]{3,2,1,0:T(8,128)(2,1)S(1)} %all_to_all.10.w0), channel_id=1, source_target_pairs={{2,0},{3,1},{4,2},{5,3},{6,4},{7,5},{8,6},{9,7},{10,8},{11,9},{12,... | collective-permute-start | bytes 3145736 | tf_op jit(solution)/shard_map/ppermute | solution.py:14
  43.8 54.1 %collective-permute-start = (bf16[16,2,128,128]{3,2,1,0:T(8,128)(2,1)S(1)}, bf16[16,2,128,128]{3,2,1,0:T(8,128)(2,1)}, u32[]{:S(2)}, u32[]{:S(2)}) collective-permute-start(bf16[16,2,128,128]{3,2,1,0:T(8,128)(2,1)S(1)} %all_to_all.10.w0), channel_id=1, source_target_pairs={{1,0},{2,1},{3,2},{4,3},{5,4},{6,5},{7,6},{8,7},{9,8},{10,9},{11,1... | collective-permute-start | bytes 3145736 | tf_op jit(solution)/shard_map/ppermute | solution.py:14
  98.0 1.0 copy-start.1

commit v2 on v1

--- a/solution.py
+++ b/solution.py
@@ -136,83 +136,296 @@
             multiply(q + 1)
         reduce(q)
 
-def mix_kernel(mix, values, out):
-    tile = out.shape[-1]
+MESH = pl.DeviceIdType.MESH
+
+
+def fused_kernel(
+    tiles,
+    offsets,
+    counts,
+    mix,
+    values,
+    weights,
+    flow,
+    choose,
+    out,
+    expected,
+    window,
+    sorted_weights,
+    results,
+    scaled,
+    chosen,
+    cont,
+    value,
+    in_send,
+    in_recv,
+    one_send,
+    one_recv,
+    two_send,
+    two_recv,
+    out_send,
+    out_recv,
+    weight_sems,
+    local_sem,
+):
+    chips = tiles // 2
+    levels, blocks, tile, _ = weights.shape
+    rows = values.shape[1]
+    me = lax.axis_index("skill")
+    chip = lax.div(me, 2)
+    core = lax.rem(me, 2)
+    partner = chip * 2 + 1 - core
+
+    def device(at):
+        return {"skill": at * 2 + core}
+
+    def source(step):
+        return lax.rem(chip + step, chips)
+
+    barrier = pltpu.get_barrier_semaphore()
+
+    def greet(step, carry):
+        pl.semaphore_signal(barrier, inc=1, device_id=device(source(step)), device_id_type=MESH)
+        return carry
+
+    lax.fori_loop(1, chips, greet, 0)
+    pl.semaphore_signal(barrier, inc=1, device_id={"skill": partner}, device_id_type=MESH)
+
     parts = split_three(mix[...])
-    for t in range(out.shape[0]):
-        block = values[:, t * tile : (t + 1) * tile]
+
+    def mixed(target, a):
+        block = values[a, :, pl.ds(pl.multiple_of(target * 2 * tile, 2 * tile), 2 * tile)]
         total = jnp.dot(parts[2], block, preferred_element_type=jnp.float32)
         total = total + jnp.dot(parts[1], block, preferred_element_type=jnp.float32)
         total = total + jnp.dot(parts[0], block, preferred_element_type=jnp.float32)
-        out[t, 0] = total.astype(jnp.bfloat16)
-
-
-def level_kernel(
-    tiles, offsets, counts, weights, flow, choose, w0, w1, w2, w3, out, sorted_weights, scaled, chosen, cont, value
-):
-    levels = weights.shape[0]
-    rows = w0.shape[2]
-    tile = w0.shape[3]
-
-    @pl.when(pl.program_id(0) == 0)
+        return total.astype(jnp.bfloat16)
+
+    def in_copy(target, origin):
+        return pltpu.make_async_remote_copy(
+            src_ref=expected.at[target],
+            dst_ref=window.at[origin, pl.ds(0, 2)],
+            send_sem=in_send.at[target],
+            recv_sem=in_recv.at[origin],
+            device_id=device(target),
+            device_id_type=MESH,
+        )
+
+    def one_copy(at):
+        return pltpu.make_async_remote_copy(
+            src_ref=window.at[at, pl.ds(0, 2)],
+            dst_ref=window.at[at, pl.ds(2, 2)],
+            send_sem=one_send.at[at],
+            recv_sem=one_recv.at[at],
+            device_id=device(lax.rem(chip + chips - 1, chips)),
+            device_id_type=MESH,
+        )
+
+    def two_copy(at):
+        return pltpu.make_async_remote_copy(
+            src_ref=window.at[at, 0],
+            dst_ref=window.at[at, 4],
+            send_sem=two_send.at[at],
+            recv_sem=two_recv.at[at],
+            device_id=device(lax.rem(chip + chips - 2, chips)),
+            device_id_type=MESH,
+        )
+
+    def out_copy(target, origin):
+        return pltpu.make_async_remote_copy(
+            src_ref=results.at[target],
+            dst_ref=out.at[pl.ds(origin * 2, 2)],
+            send_sem=out_send.at[target],
+            recv_sem=out_recv.at[origin],
+            device_id=device(target),
+            device_id_type=MESH,
+        )
+
+    def weight_copy(which):
+        return pltpu.make_async_remote_copy(
+            src_ref=sorted_weights.at[which],
+            dst_ref=sorted_weights.at[which],
+            send_sem=weight_sems.at[0],
+            recv_sem=weight_sems.at[1],
+            device_id={"skill": partner},
+            device_id_type=MESH,
+        )
+
+    pl.semaphore_wait(barrier, chips)
+
+    def send_in(step, carry):
+        target = lax.rem(chip + chips - step, chips)
+        for a in range(2):
+            total = mixed(target, a)
+            expected[target, 0, a] = total[:, :tile]
+            expected[target, 1, a] = total[:, tile:]
+        in_copy(target, chip).start()
+        return carry
+
+    lax.fori_loop(1, chips, send_in, 0)
+    for a in range(2):
+        total = mixed(chip, a)
+        window[chip, 0, a] = total[:, :tile]
+        window[chip, 1, a] = total[:, tile:]
+
+    @pl.when(chip + 1 >= chips)
     def _():
-        t = lax.axis_index("skill")
-        arrange_weights(t, tiles, weights, [offsets[0, k] for k in range(4)], counts[0, 0], sorted_weights)
-
-    window = jnp.concatenate([w[0].reshape(2 * rows, tile) for w in (w0, w1, w2, w3)], axis=1)
-    one_chunk(window, flow[...], choose[...], sorted_weights, scaled, chosen, cont, value, levels, rows)
-    for a in range(2):
-        out[0, a] = value[a].T.astype(jnp.bfloat16)
+        def clear(at, carry):
+            for slot in (2, 3):
+                window[at, slot] = jnp.zeros(window.shape[2:], jnp.bfloat16)
+            return carry
+
+        lax.fori_loop(0, chips, clear, 0)
+
+    @pl.when(chip + 2 >= chips)
+    def _():
+        def clear(at, carry):
+            window[at, 4] = jnp.zeros(window.shape[2:], jnp.bfloat16)
+            return carry
+
+        lax.fori_loop(0, chips, clear, 0)
+
+    def relay(at):
+        @pl.when(chip >= 1)
+        def _():
+            one_copy(at).start()
+
+        @pl.when(chip >= 2)
+        def _():
+            two_copy(at).start()
+
+    relay(chip)
+    arrange_weights(
+        me, tiles, weights, [offsets[0, k] for k in range(blocks)], counts[0, 0], sorted_weights.at[core]
+    )
+    weight_copy(core).start()
+
+    def arrive(step):
+        at = source(step)
+        in_copy(lax.rem(chip + 1, chips), at).wait_recv()
+        relay(at)
+
+    arrive(1)
+    arrive(2)
+    weight_copy(1 - core).wait_recv()
+
+    def compute(step, carry):
+        at = source(step + 2)
+
+        @pl.when(step + 3 < chips)
+        def _():
+            arrive(step + 3)
+
+        @pl.when(chip + 1 < chips)
+        def _():
+            one_copy(at).wait_recv()
+
+        @pl.when(chip + 2 < chips)
+        def _():
+            two_copy(at).wait_recv()
+
+        start = pl.multiple_of((at * 2 + core) * rows, rows)
+        flow_here = flow[:, :, pl.ds(start, rows)]
+        choose_here = choose[:, :, pl.ds(start, rows)]
+
+        def one_tile(t, inner):
+            blocks_here = [window[at, t + r].reshape(2 * rows, tile) for r in range(blocks)]
+            one_chunk(
+                jnp.concatenate(blocks_here, axis=1),
+                flow_here,
+                choose_here,
+                sorted_weights.at[t],
+                scaled,
+                chosen,
+                cont,
+                value,
+                levels,
+                rows,
+            )
+            for a in range(2):
+                results[at, t, a] = value[a].T.astype(jnp.bfloat16)
+            return inner
+
+        lax.fori_loop(0, 2, one_tile, 0)
+
+        @pl.when(at != chip)
+        def _():
+            out_copy(at, chip).start()
+
+        @pl.when(at == chip)
+        def _():
+            pltpu.make_async_copy(results.at[chip], out.at[pl.ds(chip * 2, 2)], local_sem).start()
+
+        return carry
+
+    lax.fori_loop(0, chips, compute, 0)
+
+    pltpu.make_async_copy(results.at[chip], out.at[pl.ds(chip * 2, 2)], local_sem).wait()
+    weight_copy(core).wait_send()
+
+    def finish(step, carry):
+        at = source(step)
+        in_copy(at, chip).wait_send()
+        out_copy(at, chip).wait_send()
+        out_copy(at, at).wait_recv()
+        return carry
+
+    lax.fori_loop(1, chips, finish, 0)
+
+    def relayed(at, carry):
+        @pl.when(chip >= 1)
+        def _():
+            one_copy(at).wait_send()
+
+        @pl.when(chip >= 2)
+        def _():
+            two_copy(at).wait_send()
+
+        return carry
+
+    lax.fori_loop(0, chips, relayed, 0)
 
 
 def on_device(value_next, income_matrix, block_weights, block_offset, block_count, asset_next, flow):
     tiles = lax.axis_size("skill")
+    chips = tiles // 2
     rows, assets, skills = value_next.shape
     tile = skills // tiles
     shocks = income_matrix.shape[0]
     levels, blocks = block_weights.shape[1:3]
     mix = jnp.kron(jnp.eye(rows // shocks, dtype=jnp.float32), income_matrix)
     turned = jnp.transpose(value_next, (1, 0, 2))
-    expected = pl.pallas_call(
-        mix_kernel,
+    smem = pl.BlockSpec(memory_space=pltpu.SMEM)
+    vmem = pl.BlockSpec(memory_space=pltpu.VMEM)
+    dma = pltpu.SemaphoreType.DMA
+    back = pl.pallas_call(
+        functools.partial(fused_kernel, tiles),
         out_shape=jax.ShapeDtypeStruct((tiles, assets, rows, tile), jnp.bfloat16),
-        grid=(assets,),
-        in_specs=[
-            pl.BlockSpec((rows, rows), lambda a: (0, 0)),
-            pl.BlockSpec((None, rows, skills), lambda a: (a, 0, 0)),
-        ],
-        out_specs=pl.BlockSpec((tiles, 1, rows, tile), lambda a: (0, a, 0, 0)),
-    )(mix, turned)
-    own = lax.all_to_all(expected, "skill", split_axis=0, concat_axis=0, tiled=True)
-    window = [own] + [shifted(own, "skill", -step) for step in range(1, blocks)]
-    chunk = pl.BlockSpec((1, assets, rows, tile), lambda n: (n, 0, 0, 0))
-    per_row = pl.BlockSpec((levels, assets, rows), lambda n: (0, 0, n))
-    value = pl.pallas_call(
-        functools.partial(level_kernel, tiles),
-        out_shape=jax.ShapeDtypeStruct((tiles, assets, rows, tile), jnp.bfloat16),
-        grid=(tiles,),
-        in_specs=[
-            pl.BlockSpec(memory_space=pltpu.SMEM),
-            pl.BlockSpec(memory_space=pltpu.SMEM),
-            pl.BlockSpec((levels, blocks, tile, tile), lambda n: (0, 0, 0, 0)),
-            per_row,
-            per_row,
-            chunk,
-            chunk,
-            chunk,
-            chunk,
-        ],
-        out_specs=chunk,
+        in_specs=[smem, smem, vmem, vmem, vmem, vmem, vmem],
+        out_specs=pl.BlockSpec(memory_space=pl.ANY),
         scratch_shapes=[
-            pltpu.VMEM((tile // STEP, levels * STEP, blocks * tile), jnp.bfloat16),
+            pltpu.VMEM((chips, 2, assets, rows, tile), jnp.bfloat16),
+            pltpu.VMEM((chips, blocks + 1, assets, rows, tile), jnp.bfloat16),
+            pltpu.VMEM((2, tile // STEP, levels * STEP, blocks * tile), jnp.bfloat16),
+            pltpu.VMEM((chips, 2, assets, rows, tile), jnp.bfloat16),
             pltpu.VMEM((assets, levels, rows), jnp.float32),
             pltpu.VMEM((assets, levels, rows), jnp.int32),
             pltpu.VMEM((2, levels * STEP, assets * rows), jnp.float32),
             pltpu.VMEM((assets, tile, rows), jnp.float32),
+            dma((chips,)),
+            dma((chips,)),
+            dma((chips,)),
+            dma((chips,)),
+            dma((chips,)),
+            dma((chips,)),
+            dma((chips,)),
+            dma((chips,)),
+            dma((2,)),
+            dma,
         ],
-        compiler_params=pltpu.CompilerParams(vmem_limit_bytes=48 * 1024 * 1024),
-    )(block_offset[0], block_count, block_weights[0], flow, asset_next, *window)
-    back = lax.all_to_all(value, "skill", split_axis=0, concat_axis=0, tiled=True)
+        compiler_params=pltpu.CompilerParams(
+            collective_id=0, has_side_effects=True, vmem_limit_bytes=48 * 1024 * 1024
+        ),
+    )(block_offset[0], block_count, mix, turned, block_weights[0], flow, asset_next)
     return jnp.transpose(back, (2, 1, 0, 3)).reshape(rows, assets, skills)
 
 
@@ -228,7 +441,7 @@
     )
 
     def body(value_next, income_matrix, *rest):
-        whole = value_next.shape[0] % income_matrix.shape[0] == 0
+        whole = value_next.shape[0] % income_matrix.shape[0] == 0 and mesh.shape["skill"] >= 8
         return (on_device if whole else on_device_split)(value_next, income_matrix, *rest)
 
     return jax.shard_map(

time: 156 us -> 95 us (0.61)
  Pallas kernels: 25.4 us -> 88.5 us
  blocking collectives: 61.8 us -> 0 us
  waiting for transfers between devices: 51.8 us -> 0 us
  starting transfers between devices: 7.56 us -> 0 us
  local copies, waits for them, and re-layouts: 7.04 us -> 5.39 us
    pallas_call x2 -> x1, Pallas kernels: 25.4 us -> 88.5 us  [on_device(): pl.pallas_call(functools.partial(fused_kernel, tiles), out_shape=jax.Shap...]
    all_to_all x2 -> x0, blocking collectives: 61.8 us -> none  [the longest x1 31.3 us: on_device(): lax.all_to_all(expected, 'skill', split_axis=0, concat_axis=0, tiled=True)]
    ppermute x3 -> x0, waiting for transfers between devices: 51.8 us -> none  [shifted(): return lax.ppermute(block, axis, route)]
    ppermute x3 -> x0, starting transfers between devices: 7.56 us -> none  [shifted(): return lax.ppermute(block, axis, route)]
    unnamed x9, local copies, waits for them, and re-layouts: 3.51 us -> 1.64 us
  transfers between devices with their start and end apart: 3 -> 0, of which waited for: 3 -> 0; matrix products, arithmetic and copies ran while one was open for 0% -> 0% of each run, Pallas kernels for 0% -> 0%
where the time goes in v2:
time: 95 us; the launch traced here: 94.8 us
  Pallas kernels  88.5 us (93%)
  local copies, waits for them, and re-layouts  5.39 us (6%)
    pallas_call x1, Pallas kernels, on_device(): pl.pallas_call(functools.partial(fused_kernel, tiles), out_shape=jax.Shap...  88.5 us
    reshape x1, local copies, waits for them, and re-layouts, on_device(): return jnp.transpose(back, (2, 1, 0, 3)).reshape(rows, assets, skills)  2.01 us

profile of v2, /device:TPU:16, one launch (start us, length us, event | category | flops | bytes accessed | tf_op | source)
XLA Modules:
  0.0 94.8 jit_solution(8208031904143437109)
XLA Ops:
  0.0 0.0 copy-start.1
  0.0 0.0 copy-start.3
  0.0 0.0 copy-start
  0.0 0.9 copy.11.offsets
  0.9 0.8 broadcast_multiply_fusion
  1.8 0.2 mul.27.mix
  1.9 0.0 copy-start.2
  1.9 1.6 %copy.15 = bf16[128,2,2048]{2,0,1:T(8,128)(2,1)S(1)} copy(bf16[128,2,2048]{2,1,0:T(2,128)(2,1)} %param.7) | data formatting | bytes 2097152 | tf_op args[0]
  3.6 0.0 copy-done.1
  3.6 0.0 copy-done.3
  3.6 0.0 copy-done
  3.6 0.0 copy-done.2
  3.6 88.5 %shard_map.73 = bf16[16,2,128,128]{3,2,1,0:T(8,128)(2,1)S(1)} custom-call(s32[16,4]{1,0:T(8,128)S(1)} %copy.11.offsets, s32[1,16]{1,0:T(1,128)S(1)} %copy-done.3, f32[128,128]{1,0:T(8,128)S(1)} %mul.27.mix, bf16[2,128,2048]{2,1,0:T(8,128)(2,1)S(1)} %bitcast.8, bf16[16,4,128,128]{3,2,1,0:T(8,128)(2,1)S(1)} %bitcast.9, f32[16,2,2048]{2,1,0:T(2,128)S(1)} %copy-done.1, ...), custom_call_target="tpu_custom_call" | custom-call | tf_op jit(solution)/shard_map/pallas_call | solution.py:400
  92.1 0.7 copy.12
  92.8 2.0 %copy.13 = bf16[128,2,2048]{2,1,0:T(2,128)(2,1)} copy(bf16[128,2,2048]{0,2,1:T(8,128)(2,1)S(1)} %bitcast.10) | data formatting | bytes 2097152 | tf_op jit(solution)/shard_map/reshape | solution.py:429
  (1 shorter events, 0.0 us)
Async XLA Ops:
  0.0 3.6 %copy-start.1 = (f32[16,2,2048]{2,1,0:T(2,128)S(1)}, f32[16,2,2048]{2,1,0:T(2,128)}, u32[]{:S(2)}) copy-start(f32[16,2,2048]{2,1,0:T(2,128)} %flow.1) | copy-start | bytes 786436
  0.0 3.6 %copy-start.3 = (s32[1,16]{1,0:T(1,128)S(1)}, s32[1,16]{1,0:T(1,128)}, u32[]{:S(2)}) copy-start(s32[1,16]{1,0:T(1,128)} %counts.1) | copy-start | bytes 196
  0.0 3.6 %copy-start = (bf16[1,16,4,128,128]{4,3,2,1,0:T(8,128)(2,1)S(1)}, bf16[1,16,4,128,128]{4,3,2,1,0:T(8,128)(2,1)}, u32[]{:S(2)}) copy-start(bf16[1,16,4,128,128]{4,3,2,1,0:T(8,128)(2,1)} %param.9) | copy-start | bytes 6291460
  1.9 1.7 %copy-start.2 = (s32[16,2,2048]{2,1,0:T(2,128)S(1)}, s32[16,2,2048]{2,1,0:T(2,128)}, u32[]{:S(2)}) copy-start(s32[16,2,2048]{2,1,0:T(2,128)} %choose.1) | copy-start | bytes 786436
